TPU v7x, 32 devices: a whole 2x2x4 slice. The times are simulated.
32 devices in a mesh: context: 2 (over core), fheads: 4 (over y, x), seqs: 4 (over z).
Axes of the slice: x: 2, y: 2, z: 4, core: 2. Of those that a mesh axis runs over, the one named last changes fastest.
Arguments:
- query_rows: bfloat16 [4096, 3072], P(('seqs', 'context'), 'fheads'), parts along dimension 0, may hold values from -5 to 5
- key_rows: bfloat16 [4096, 3072], P(('seqs', 'context'), 'fheads'), parts along dimension 0, may hold values from -5 to 5
- value_rows: bfloat16 [4096, 3072], P(('seqs', 'context'), 'fheads'), parts along dimension 0, may hold values from -10 to 10
- step_sizes: float32 [4096, 4], P(('seqs', 'context'), 'fheads'), parts along dimension 0, may hold values from 2e-05 to 0.0018
- w_gate: bfloat16 [4, 768, 768], P('fheads', 'context'), may hold values from -4 to 4
- w_up: bfloat16 [4, 768, 768], P('fheads', 'context'), may hold values from -4 to 4
- w_down: bfloat16 [4, 768, 768], P('fheads', 'context'), may hold values from -4 to 4
Outputs:
- window_out: bfloat16 [4096, 3072], P(('seqs', 'context'), 'fheads'), parts along dimension 0
- fast_out: bfloat16 [4096, 3072], P(('seqs', 'context'), 'fheads'), parts along dimension 0
There are 4 independent parts, one for each index of `seqs`. A program takes and returns all parts, laid end to end along the dimension named above; an argument that names none is the same for every part. Nothing has to cross between parts.
All inputs are finite; a program needn't handle non-finite values.
Results may differ from a plain program's by a relative error of at most 0.035.
Values may be sent and summed in bfloat16 or wider, within the bound.
No kernel may reach another device: no remote copies, remote signals or barrier semaphores. Data moves between devices by JAX's collectives and lax.ppermute only.
A program may use at most 128 MiB of HBM per device.

v0:
```python
import math
import jax
import jax.numpy as jnp
from jax import lax
from jax.sharding import PartitionSpec as P

HD = 128
WINDOW = 512


def passed_along(x, axis, by):
    peers = lax.axis_size(axis)
    pairs = [(i, i + by) for i in range(peers) if 0 <= i + by < peers]
    return lax.ppermute(x, axis, pairs)


def unit_rows(values):
    return values * lax.rsqrt(jnp.mean(values * values, axis=-1, keepdims=True) + 1e-06)


def window_block(queries, keys_near, values_near, first_pos):
    row_count = queries.shape[0]
    query_pos = first_pos + jnp.arange(row_count, dtype=jnp.int32)
    key_pos = first_pos - WINDOW + jnp.arange(row_count + WINDOW, dtype=jnp.int32)
    allowed = (
        (key_pos[None, :] >= 0)
        & (key_pos[None, :] <= query_pos[:, None])
        & (key_pos[None, :] > query_pos[:, None] - WINDOW)
    )
    scores = jnp.einsum(
        "ihd,jhd->hij", queries, keys_near, preferred_element_type=jnp.float32
    ) / math.sqrt(HD)
    scores = jnp.where(allowed[None], scores, -1e30)
    row_max = jnp.max(scores, axis=-1, keepdims=True)
    powers = jnp.exp(scores - row_max)
    weights = (powers / jnp.sum(powers, axis=-1, keepdims=True)).astype(jnp.bfloat16)
    attended = jnp.einsum("hij,jhd->ihd", weights, values_near, preferred_element_type=jnp.float32)
    return attended.astype(jnp.bfloat16)


def dot_rows(first_op, second_op):
    return lax.dot_general(
        first_op, second_op, (((0,), (0,)), ((), ())), preferred_element_type=jnp.float32
    )


def dot_back(first_op, second_op):
    return lax.dot_general(
        first_op, second_op, (((1,), (1,)), ((), ())), preferred_element_type=jnp.float32
    )


def renormed(weight, gradient):
    initial = weight.astype(jnp.float32)
    fresh_rows = initial - gradient
    old_ms = jnp.mean(initial * initial, axis=0)
    new_ms = jnp.mean(fresh_rows * fresh_rows, axis=0)
    return (fresh_rows * jnp.sqrt(old_ms) * lax.rsqrt(new_ms + 1e-06)).astype(jnp.bfloat16)


def apply_fast(fast_queries, gate_w, up_w, down_w):
    gate_new = jnp.dot(fast_queries, gate_w, preferred_element_type=jnp.float32)
    up_new = jnp.dot(fast_queries, up_w, preferred_element_type=jnp.float32)
    hidden_new = (gate_new * jax.nn.sigmoid(gate_new) * up_new).astype(jnp.bfloat16)
    return jnp.dot(hidden_new, down_w, preferred_element_type=jnp.float32).astype(jnp.bfloat16)


def body(query_rows, key_rows, value_rows, step_sizes, w_gate, w_up, w_down):
    row_count = query_rows.shape[0]
    heads_here = query_rows.shape[1] // HD
    rim_keys, rim_values = passed_along((key_rows, value_rows), "context", 1)
    first_pos = lax.axis_index("context") * row_count
    keys_near = jnp.concatenate([rim_keys, key_rows], axis=0).reshape(
        row_count + WINDOW, heads_here, HD
    )
    values_near = jnp.concatenate([rim_values, value_rows], axis=0).reshape(
        row_count + WINDOW, heads_here, HD
    )
    window_out = window_block(
        query_rows.reshape(row_count, heads_here, HD), keys_near, values_near, first_pos
    )
    window_out = window_out.reshape(row_count, heads_here * HD)
    gathered = (
        lax.all_gather(w_gate, "context", axis=1, tiled=True),
        lax.all_gather(w_up, "context", axis=1, tiled=True),
        lax.all_gather(w_down, "context", axis=1, tiled=True),
    )
    gate_w = gathered[0][0]
    up_w = gathered[1][0]
    down_w = gathered[2][0]
    fast_keys = unit_rows(key_rows.astype(jnp.float32)).astype(jnp.bfloat16)
    fast_queries = unit_rows(query_rows.astype(jnp.float32)).astype(jnp.bfloat16)
    target = (-(step_sizes * value_rows.astype(jnp.float32))).astype(jnp.bfloat16)
    gate_pre = jnp.dot(fast_keys, gate_w, preferred_element_type=jnp.float32)
    up_pre = jnp.dot(fast_keys, up_w, preferred_element_type=jnp.float32)
    sigmoid_gate = jax.nn.sigmoid(gate_pre)
    hidden = (gate_pre * sigmoid_gate * up_pre).astype(jnp.bfloat16)
    back_grad = dot_back(target, down_w)
    d_gate = (back_grad * up_pre * sigmoid_gate * (1.0 + gate_pre * (1.0 - sigmoid_gate))).astype(
        jnp.bfloat16
    )
    d_up = (back_grad * gate_pre * sigmoid_gate).astype(jnp.bfloat16)
    grad_gate = dot_rows(fast_keys, d_gate)
    grad_up = dot_rows(fast_keys, d_up)
    grad_down = dot_rows(hidden, target)
    summed = (
        lax.psum(grad_gate.astype(jnp.bfloat16), "context").astype(jnp.float32),
        lax.psum(grad_up.astype(jnp.bfloat16), "context").astype(jnp.float32),
        lax.psum(grad_down.astype(jnp.bfloat16), "context").astype(jnp.float32),
    )
    updated_gate = renormed(gate_w, summed[0])
    updated_up = renormed(up_w, summed[1])
    updated_down = renormed(down_w, summed[2])
    fast_out = apply_fast(fast_queries, updated_gate, updated_up, updated_down)
    return (window_out, fast_out)


def solution(mesh):
    in_specs = (
        P(("seqs", "context"), "fheads"),
        P(("seqs", "context"), "fheads"),
        P(("seqs", "context"), "fheads"),
        P(("seqs", "context"), "fheads"),
        P("fheads", "context", None),
        P("fheads", "context", None),
        P("fheads", "context", None),
    )
    out_specs = (P(("seqs", "context"), "fheads"), P(("seqs", "context"), "fheads"))
    return jax.shard_map(body, mesh=mesh, in_specs=in_specs, out_specs=out_specs, check_vma=False)
```

profile of v0, /device:TPU:0, one launch (start us, length us, event | category | flops | bytes accessed | tf_op | source)
XLA Modules:
  0.0 101.0 jit_solution(16830201598666049020)
XLA Ops:
  7.2 0.7 all-gather.4.cloned.1.call-update
  8.0 0.7 all-gather.8.cloned.1.call-update
  8.7 0.3 copy.14
  9.0 3.3 %collective-permute-start.1 = (bf16[512,768]{0,1:T(8,128)(2,1)S(1)}, bf16[512,768]{0,1:T(8,128)(2,1)}, u32[]{:S(2)}, u32[]{:S(2)}) collective-permute-start(bf16[512,768]{0,1:T(8,128)(2,1)S(1)} %copy.14), channel_id=1, source_target_pairs={{0,16},{1,17},{2,18},{3,19},{4,20},{5,21},{6,22},{7,23},{8,24},{9,... | collective-permute-start | bytes 2359304 | tf_op jit(solution)/shard_map/ppermute | solution.py:14
  12.3 2.2 %collective-permute-start = (bf16[512,768]{1,0:T(8,128)(2,1)S(1)}, bf16[512,768]{1,0:T(8,128)(2,1)}, u32[]{:S(2)}, u32[]{:S(2)}) collective-permute-start(bf16[512,768]{1,0:T(8,128)(2,1)S(1)} %copy-done.7), channel_id=1, source_target_pairs={{0,16},{1,17},{2,18},{3,19},{4,20},{5,21},{6,22},{7,23},{8,24},{9,... | collective-permute-start | bytes 2359304 | tf_op jit(solution)/shard_map/ppermute | solution.py:14
  14.5 0.2 fusion.11
  14.8 6.7 %all-gather.4.cloned.1.call-done = bf16[1,768,768]{2,1,0:T(8,128)(2,1)} async-done(((bf16[1,384,768]{2,1,0:T(8,128)(2,1)}), bf16[1,768,768]{2,1,0:T(8,128)(2,1)}) %all-gather.4.cloned.1.call-update) | async-done | bytes 1179664 | tf_op jit(solution)/shard_map/all_gather | solution.py:84
  21.5 3.3 %fusion.21 = f32[512,768]{1,0:T(8,128)} fusion(bf16[1,768,768]{2,1,0:T(8,128)(2,1)} %all-gather.4.cloned.1.call-done, bf16[512,768]{1,0:T(8,128)(2,1)S(1)} %copy-done, f32[512]{0:T(512)S(1)} %add_rsqrt_fusion.3), kind=kOutput, calls=%fused_computation.53 | convolution fusion | flops 605159424 | bytes 3540992 | tf_op jit(solution)/shard_map/dot_general | solution.py:94
  24.8 8.7 %all-gather.8.cloned.1.call-done = bf16[1,768,768]{2,1,0:T(8,128)(2,1)} async-done(((bf16[1,384,768]{2,1,0:T(8,128)(2,1)}), bf16[1,768,768]{2,1,0:T(8,128)(2,1)}) %all-gather.8.cloned.1.call-update) | async-done | bytes 1179664 | tf_op jit(solution)/shard_map/all_gather | solution.py:85
  33.5 2.2 %fusion.16 = f32[512,768]{1,0:T(8,128)S(1)} fusion(bf16[1,768,768]{2,1,0:T(8,128)(2,1)} %all-gather.8.cloned.1.call-done, bf16[512,768]{1,0:T(8,128)(2,1)S(1)} %copy-done, f32[512]{0:T(512)S(1)} %add_rsqrt_fusion.3), kind=kOutput, calls=%fused_computation.48 | convolution fusion | flops 605159424 | bytes 3540992 | tf_op jit(solution)/shard_map/dot_general | solution.py:95
  35.7 1.1 %copy-done.11 = f32[512,768]{1,0:T(8,128)} copy-done((f32[512,768]{1,0:T(8,128)}, f32[512,768]{1,0:T(8,128)S(1)}, u32[]{:S(2)}) %copy-start.11) | copy-done | bytes 1572888
  36.9 2.1 %convolution_convert_fusion = bf16[768,768]{1,0:T(8,128)(2,1)} fusion(f32[512,768]{1,0:T(8,128)S(1)} %fusion.16, f32[512,768]{1,0:T(8,128)S(1)} %copy-done.9, bf16[512,768]{1,0:T(8,128)(2,1)S(1)} %copy-done.7, f32[512]{0:T(512)S(1)} %bitcast.56), kind=kOutput, calls=%fused_computation.41 | convolution fusion | flops 608501760 | bytes 5113856 | tf_op jit(solution)/shard_map/dot_general | solution.py:42
  39.0 6.5 %all-gather.6.cloned.1.call-done = bf16[1,768,768]{2,1,0:T(8,128)(2,1)} async-done(((bf16[1,384,768]{2,1,0:T(8,128)(2,1)}), bf16[1,768,768]{2,1,0:T(8,128)(2,1)}) %all-gather.6.cloned.1.call-update) | async-done | bytes 1179664 | tf_op jit(solution)/shard_map/all_gather | solution.py:86
  45.5 2.3 %fusion.19 = f32[512,768]{1,0:T(8,128)S(1)} fusion(bf16[1,768,768]{2,1,0:T(8,128)(2,1)} %all-gather.6.cloned.1.call-done, bf16[512,768]{1,0:T(8,128)(2,1)S(1)} %copy-done.7, f32[512]{0:T(512)S(1)} %bitcast.57), kind=kOutput, calls=%fused_computation.51 | convolution fusion | flops 605552640 | bytes 3540992 | tf_op jit(solution)/shard_map/dot_general | solution.py:48
  47.7 2.2 %convolution_convert_fusion.2 = bf16[768,768]{1,0:T(8,128)(2,1)} fusion(f32[512,768]{1,0:T(8,128)S(1)} %copy-done.10, f32[512,768]{1,0:T(8,128)S(1)} %fusion.19, f32[512,768]{1,0:T(8,128)S(1)} %copy-done.12, bf16[512,768]{1,0:T(8,128)(2,1)S(1)} %copy-done, f32[512]{0:T(512)S(1)} %add_rsqrt_fusion.3), kind=kOutput, calls=%fused_computation.43 | convolution fusion | flops 609681408 | bytes 6686720 | tf_op jit(solution)/shard_map/dot_general | solution.py:42
  50.0 2.1 %convolution_convert_fusion.1 = bf16[768,768]{1,0:T(8,128)(2,1)} fusion(f32[512,768]{1,0:T(8,128)S(1)} %fusion.19, f32[512,768]{1,0:T(8,128)S(1)} %copy-done.10, bf16[512,768]{1,0:T(8,128)(2,1)S(1)} %copy-done, f32[512]{0:T(512)S(1)} %add_rsqrt_fusion.3), kind=kOutput, calls=%fused_computation.42 | convolution fusion | flops 608108544 | bytes 5113856 | tf_op jit(solution)/shard_map/dot_general | solution.py:42
  52.1 1.1 %copy-done.1 = bf16[512,768]{1,0:T(8,128)(2,1)S(1)} copy-done((bf16[512,768]{1,0:T(8,128)(2,1)S(1)}, bf16[512,768]{1,0:T(8,128)(2,1)}, u32[]{:S(2)}) %copy-start.1) | copy-done | bytes 786456
  53.2 1.2 %copy.16 = bf16[512,768]{0,1:T(8,128)(2,1)} copy(bf16[512,768]{1,0:T(8,128)(2,1)S(1)} %copy-done.1) | data formatting | bytes 1572864 | tf_op args[0]
  54.4 0.2 fusion.9
  54.6 1.8 %compare_and_fusion = pred[512,1024]{0,1:T(8,128)(4,1)} fusion(s32[512]{0:T(512)S(1)} %get-tuple-element.18, s32[512]{0:T(512)S(1)} %get-tuple-element.17, s32[1024]{0:T(1024)S(1)} %iota_add_fusion, pred[1024]{0:T(1024)(128)(4,1)S(1)} %broadcast_compare_fusion), kind=kLoop, calls=%fused_computation.24 | loop fusion | flops 2097152 | bytes 533504 | tf_op jit(solution)/shard_map/and | solution.py:26
  56.4 1.5 %pad_maximum_fusion = bf16[1024,768]{1,0:T(8,128)(2,1)S(1)} fusion(bf16[512,768]{1,0:T(8,128)(2,1)} %param.9, bf16[512,768]{1,0:T(8,128)(2,1)} %collective-permute-done), kind=kLoop, calls=%fused_computation.33 | loop fusion | flops 3145728 | bytes 3145728 | tf_op jit(solution)/shard_map/concatenate | solution.py:76
  57.9 1.7 %copy.13 = bf16[1024,768]{0,1:T(8,128)(2,1)} copy(bf16[1024,768]{1,0:T(8,128)(2,1)S(1)} %pad_maximum_fusion) | data formatting | bytes 3145728 | tf_op jit(solution)/shard_map/concatenate | solution.py:76
  59.5 2.8 %pad_maximum_fusion.1 = bf16[1024,768]{0,1:T(8,128)(2,1)} fusion(bf16[512,768]{0,1:T(8,128)(2,1)S(1)} %copy.14, bf16[512,768]{0,1:T(8,128)(2,1)} %collective-permute-done.1), kind=kLoop, calls=%fused_computation.34 | loop fusion | flops 3145728 | bytes 3145728 | tf_op jit(solution)/shard_map/concatenate | solution.py:73
  62.3 12.6 %fusion.45 = (f32[6,512]{1,0:T(8,128)S(1)}, f32[6,512,1024]{1,2,0:T(8,128)}) fusion(pred[512,1024]{0,1:T(8,128)(4,1)} %compare_and_fusion, bf16[1024,6,128]{0,2,1:T(8,128)(2,1)} %bitcast.53, bf16[512,6,128]{0,2,1:T(8,128)(2,1)} %bitcast.54), kind=kOutput, calls=%fused_computation.81 | convolution fusion | flops 817890304 | bytes 15478784 | tf_op jit(solution)/shard_map/sub | solution.py:35
  74.9 6.0 %fusion.13 = bf16[6,128,512]{2,1,0:T(8,128)(2,1)S(1)} fusion(bf16[1024,6,128]{0,2,1:T(8,128)(2,1)S(1)} %bitcast.52, f32[6,512,1024]{1,2,0:T(8,128)} %get-tuple-element.16, f32[6,512]{1,0:T(8,128)S(1)} %get-tuple-element.15), kind=kOutput, calls=%fused_computation.45 | convolution fusion | flops 811991040 | bytes 14954496 | tf_op jit(solution)/shard_map/hij,jhd->ihd/dot_general | solution.py:37
  80.9 1.2 %copy.20 = bf16[512,768]{1,0:T(8,128)(2,1)} copy(bf16[512,768]{0,1:T(8,128)(2,1)S(1)} %bitcast.55) | data formatting | bytes 1572864
  82.1 3.6 %fusion.6 = (f32[768]{0:T(1024)S(1)}, f32[768]{0:T(1024)S(1)}, f32[768]{0:T(1024)S(1)}, f32[768]{0:T(1024)S(1)}) fusion(bf16[1,768,768]{2,1,0:T(8,128)(2,1)} %all-gather.4.cloned.1.call-done, bf16[768,768]{1,0:T(8,128)(2,1)} %get-tuple-element.13, bf16[768,768]{1,0:T(8,128)(2,1)} %get-tuple-element.14, bf16[1,768,768]{2,1,0:T(8,128)(2,1)} %all-gather.8.cloned.1.call-done), kind=kLoop, calls=%fused_computation.15 | loop fusion | flops 8254464 | bytes 4730880 | tf_op jit(solution)/shard_map/reduce_sum | solution.py:56
  85.7 0.6 fusion.8
  86.3 0.6 copy-done.5
  86.9 0.4 copy-done.6
  87.3 2.1 %fusion.14 = f32[512,768]{1,0:T(8,128)} fusion(bf16[768,768]{1,0:T(8,128)(2,1)S(1)} %copy-done.6, bf16[1,768,768]{2,1,0:T(8,128)(2,1)S(1)} %copy-done.5, f32[768]{0:T(1024)S(1)} %add_rsqrt_fusion.2, f32[768]{0:T(1024)S(1)} %multiply_sqrt_fusion.2, bf16[512,768]{1,0:T(8,128)(2,1)S(1)} %copy-done.1, f32[512]{0:T(512)S(1)} %add_rsqrt_fusion.4), kind=kOutput, calls=%fused_computation.46 | convolution fusion | flops 608698368 | bytes 4726784 | tf_op jit(solution)/shard_map/dot_general | solution.py:62
  89.4 5.1 %convolution_convert_fusion.3 = bf16[512,768]{1,0:T(8,128)(2,1)} fusion(bf16[768,768]{1,0:T(8,128)(2,1)} %get-tuple-element.12, bf16[1,768,768]{2,1,0:T(8,128)(2,1)S(1)} %copy-done.3, f32[768]{0:T(1024)S(1)} %get-tuple-element.21, f32[768]{0:T(1024)S(1)} %get-tuple-element.22, f32[512,768]{1,0:T(8,128)} %fusion.14, bf16[768,768]{1,0:T(8,128)(2,1)} %get-tuple-element.14, ...), kind=kOutput, calls=%fused_computation.44 | convolution fusion | flops 1218969600 | bytes 7878656 | tf_op jit(solution)/shard_map/dot_general | solution.py:65
  (41 shorter events, 0.3 us)
Async XLA Ops:
  7.2 1.6 %copy-start = (bf16[512,768]{1,0:T(8,128)(2,1)S(1)}, bf16[512,768]{1,0:T(8,128)(2,1)}, u32[]{:S(2)}) copy-start(bf16[512,768]{1,0:T(8,128)(2,1)} %param.8) | copy-start | bytes 2359300
  7.2 5.1 %copy-start.7 = (bf16[512,768]{1,0:T(8,128)(2,1)S(1)}, bf16[512,768]{1,0:T(8,128)(2,1)}, u32[]{:S(2)}) copy-start(bf16[512,768]{1,0:T(8,128)(2,1)} %param.9) | copy-start | bytes 2359300
  7.2 14.3 %all-gather.4.cloned.1.call-start = ((), (), s32[]{:S(2)}) async-start(), calls=%async_computation | async-start | bytes 1769472 | tf_op jit(solution)/shard_map/all_gather | solution.py:84
  7.9 25.6 %all-gather.8.cloned.1.call-start = ((), (), s32[]{:S(2)}) async-start(), calls=%async_computation.2 | async-start | bytes 1769472 | tf_op jit(solution)/shard_map/all_gather | solution.py:85
  8.7 36.8 %all-gather.6.cloned.1.call-start = ((), (), s32[]{:S(2)}) async-start(), calls=%async_computation.1 | async-start | bytes 1769472 | tf_op jit(solution)/shard_map/all_gather | solution.py:86
  9.0 50.5 %collective-permute-start.1 = (bf16[512,768]{0,1:T(8,128)(2,1)S(1)}, bf16[512,768]{0,1:T(8,128)(2,1)}, u32[]{:S(2)}, u32[]{:S(2)}) collective-permute-start(bf16[512,768]{0,1:T(8,128)(2,1)S(1)} %copy.14), channel_id=1, source_target_pairs={{0,16},{1,17},{2,18},{3,19},{4,20},{5,21},{6,22},{7,23},{8,24},{9,... | collective-permute-start | bytes 2359304 | tf_op jit(solution)/shard_map/ppermute | solution.py:14
  12.3 44.1 %collective-permute-start = (bf16[512,768]{1,0:T(8,128)(2,1)S(1)}, bf16[512,768]{1,0:T(8,128)(2,1)}, u32[]{:S(2)}, u32[]{:S(2)}) collective-permute-start(bf16[512,768]{1,0:T(8,128)(2,1)S(1)} %copy-done.7), channel_id=1, source_target_pairs={{0,16},{1,17},{2,18},{3,19},{4,20},{5,21},{6,22},{7,23},{8,24},{9,... | collective-permute-start | bytes 2359304 | tf_op jit(solution)/shard_map/ppermute | solution.py:14
  14.5 67.6 %all-reduce.3.cloned.1.call-start = ((), (), s32[]{:S(2)}) async-start(), calls=%async_computation.3 | async-start | bytes 7077888 | tf_op jit(solution)/shard_map/psum | solution.py:109
  24.8 12.1 %copy-start.8 = (f32[512,1]{0,1:T(1,128)S(1)}, f32[512,1]{0,1:T(1,128)}, u32[]{:S(2)}) copy-start(f32[512,1]{0,1:T(1,128)} %param.10) | copy-start | bytes 6148
  33.5 3.4 %copy-start.9 = (f32[512,768]{1,0:T(8,128)S(1)}, f32[512,768]{1,0:T(8,128)}, u32[]{:S(2)}) copy-start(f32[512,768]{1,0:T(8,128)} %fusion.21) | copy-start | bytes 4718596
  35.7 1.1 %copy-start.11 = (f32[512,768]{1,0:T(8,128)}, f32[512,768]{1,0:T(8,128)S(1)}, u32[]{:S(2)}) copy-start(f32[512,768]{1,0:T(8,128)S(1)} %fusion.16) | copy-start | bytes 4718596
  45.5 2.3 %copy-start.10 = (f32[512,768]{1,0:T(8,128)S(1)}, f32[512,768]{1,0:T(8,128)}, u32[]{:S(2)}) copy-start(f32[512,768]{1,0:T(8,128)} %fusion.21) | copy-start | bytes 4718596
  45.5 2.3 %copy-start.12 = (f32[512,768]{1,0:T(8,128)S(1)}, f32[512,768]{1,0:T(8,128)}, u32[]{:S(2)}) copy-start(f32[512,768]{1,0:T(8,128)} %copy-done.11) | copy-start | bytes 4718596
  52.1 1.1 %copy-start.1 = (bf16[512,768]{1,0:T(8,128)(2,1)S(1)}, bf16[512,768]{1,0:T(8,128)(2,1)}, u32[]{:S(2)}) copy-start(bf16[512,768]{1,0:T(8,128)(2,1)} %param.7) | copy-start | bytes 2359300
  62.3 12.6 %copy-start.2 = (bf16[1024,768]{0,1:T(8,128)(2,1)S(1)}, bf16[1024,768]{0,1:T(8,128)(2,1)}, u32[]{:S(2)}) copy-start(bf16[1024,768]{0,1:T(8,128)(2,1)} %copy.13) | copy-start | bytes 4718596
  82.1 3.7 %copy-start.3 = (bf16[1,768,768]{2,1,0:T(8,128)(2,1)S(1)}, bf16[1,768,768]{2,1,0:T(8,128)(2,1)}, u32[]{:S(2)}) copy-start(bf16[1,768,768]{2,1,0:T(8,128)(2,1)} %all-gather.6.cloned.1.call-done) | copy-start | bytes 3538948
  82.1 3.7 %copy-start.4 = (bf16[768,768]{1,0:T(8,128)(2,1)S(1)}, bf16[768,768]{1,0:T(8,128)(2,1)}, u32[]{:S(2)}) copy-start(bf16[768,768]{1,0:T(8,128)(2,1)} %get-tuple-element.12) | copy-start | bytes 3538948
  85.7 1.3 %copy-start.5 = (bf16[1,768,768]{2,1,0:T(8,128)(2,1)S(1)}, bf16[1,768,768]{2,1,0:T(8,128)(2,1)}, u32[]{:S(2)}) copy-start(bf16[1,768,768]{2,1,0:T(8,128)(2,1)} %all-gather.4.cloned.1.call-done) | copy-start | bytes 3538948
  85.7 1.6 %copy-start.6 = (bf16[768,768]{1,0:T(8,128)(2,1)S(1)}, bf16[768,768]{1,0:T(8,128)(2,1)}, u32[]{:S(2)}) copy-start(bf16[768,768]{1,0:T(8,128)(2,1)} %get-tuple-element.13) | copy-start | bytes 3538948
Sparse Core Ops, SparseCore 0:
  9.5 11.9 all-gather.3
  23.1 10.3 all-gather.7
  35.0 10.3 all-gather.5
  52.2 25.4 all-reduce.2
where the time goes:
time: 101 us
  matrix products  40 us (40%)
  waiting for transfers between devices  23.3 us (23%)
  between operations  14 us (14%)
  other arithmetic  10.7 us (11%)
  local copies, waits for them, and re-layouts  7.44 us (7%)
  starting transfers between devices  5.59 us (6%)
    sub x1, matrix products, window_block(): powers = jnp.exp(scores - row_max)  12.6 us
    all_gather x1, waiting for transfers between devices, body(): lax.all_gather(w_up, 'context', axis=1, tiled=True)  8.71 us
    all_gather x1, waiting for transfers between devices, body(): lax.all_gather(w_gate, 'context', axis=1, tiled=True)  6.74 us
    all_gather x1, waiting for transfers between devices, body(): lax.all_gather(w_down, 'context', axis=1, tiled=True)  6.47 us
    dot_general x3, matrix products, dot_rows(): lax.dot_general(first_op, second_op, (((0,), (0,)), ((), ())), preferred_...  6.46 us
    dot_general x1, matrix products, window_block(): jnp.einsum('hij,jhd->ihd', weights, values_near, preferred_element_type=j...  6.05 us
    unnamed x29, local copies, waits for them, and re-layouts  5.79 us
    ppermute x2, starting transfers between devices, passed_along(): return lax.ppermute(x, axis, pairs)  5.44 us
  transfers between devices with their start and end apart: 6, of which 3 were waited for; matrix products, arithmetic and copies ran while one was open for 43% of the time, Pallas kernels for 0%

commit v1 on v0

--- a/solution.py
+++ b/solution.py
@@ -81,7 +81,7 @@
     )
     window_out = window_out.reshape(row_count, heads_here * HD)
     gathered = (
-        lax.all_gather(w_gate, "context", axis=1, tiled=True),
+        jnp.concatenate(lax.all_gather(w_gate, "context"), axis=1),
         lax.all_gather(w_up, "context", axis=1, tiled=True),
         lax.all_gather(w_down, "context", axis=1, tiled=True),
     )

time: 101 us -> 99.4 us (0.984)
  local copies, waits for them, and re-layouts: 7.44 us -> 5.9 us
    reduce_sum x0 -> x1, other arithmetic: none -> 1.84 us  [renormed(): new_ms = jnp.mean(fresh_rows * fresh_rows, axis=0)]
    unnamed x29 -> x33, local copies, waits for them, and re-layouts: 5.79 us -> 4.24 us
    sub x1, matrix products: 12.6 us -> 11.1 us  [window_block(): powers = jnp.exp(scores - row_max)]
    reduce_sum x2, other arithmetic: 4.14 us -> 2.74 us  [renormed(): old_ms = jnp.mean(initial * initial, axis=0)]
    dot_general x1, matrix products: 6.05 us -> 7.21 us  [window_block(): jnp.einsum('hij,jhd->ihd', weights, values_near, preferred_element_type=j...]
  transfers between devices with their start and end apart: 6 -> 6, of which waited for: 3 -> 3; matrix products, arithmetic and copies ran while one was open for 43% -> 44% of each run, Pallas kernels for 0% -> 0%
where the time goes in v1:
time: 99.4 us; the launch traced here: 99 us
  matrix products  39.7 us (40%)
  waiting for transfers between devices  23 us (23%)
  between operations  14 us (14%)
  other arithmetic  10.7 us (11%)
  local copies, waits for them, and re-layouts  5.9 us (6%)
  starting transfers between devices  5.6 us (6%)
    sub x1, matrix products, window_block(): powers = jnp.exp(scores - row_max)  11.1 us
    all_gather x1, waiting for transfers between devices, body(): lax.all_gather(w_up, 'context', axis=1, tiled=True)  8.71 us
    dot_general x1, matrix products, window_block(): jnp.einsum('hij,jhd->ihd', weights, values_near, preferred_element_type=j...  7.21 us
    dot_general x3, matrix products, dot_rows(): lax.dot_general(first_op, second_op, (((0,), (0,)), ((), ())), preferred_...  6.49 us
    all_gather x1, waiting for transfers between devices, body(): lax.all_gather(w_gate, 'context')  6.46 us
    all_gather x1, waiting for transfers between devices, body(): lax.all_gather(w_down, 'context', axis=1, tiled=True)  6.44 us
    ppermute x2, starting transfers between devices, passed_along(): return lax.ppermute(x, axis, pairs)  5.44 us
    dot_general x1, matrix products, apply_fast(): jnp.dot(hidden_new, down_w, preferred_element_type=jnp.float32)  5.05 us
  transfers between devices with their start and end apart: 6, of which 3 were waited for; matrix products, arithmetic and copies ran while one was open for 44% of the time, Pallas kernels for 0%

profile of v1, /device:TPU:0, one launch (start us, length us, event | category | flops | bytes accessed | tf_op | source)
XLA Modules:
  0.0 99.0 jit_solution(17460609381326047368)
XLA Ops:
  7.2 0.7 all-gather.9.cloned.1.call-update
  8.0 0.7 all-gather.7.cloned.1.call-update
  8.7 0.3 copy.22
  9.0 3.3 %collective-permute-start.1 = (bf16[512,768]{0,1:T(8,128)(2,1)S(1)}, bf16[512,768]{0,1:T(8,128)(2,1)}, u32[]{:S(2)}, u32[]{:S(2)}) collective-permute-start(bf16[512,768]{0,1:T(8,128)(2,1)S(1)} %copy.22), channel_id=1, source_target_pairs={{0,16},{1,17},{2,18},{3,19},{4,20},{5,21},{6,22},{7,23},{8,24},{9,... | collective-permute-start | bytes 2359304 | tf_op jit(solution)/shard_map/ppermute | solution.py:14
  12.3 2.2 %collective-permute-start = (bf16[512,768]{1,0:T(8,128)(2,1)S(1)}, bf16[512,768]{1,0:T(8,128)(2,1)}, u32[]{:S(2)}, u32[]{:S(2)}) collective-permute-start(bf16[512,768]{1,0:T(8,128)(2,1)S(1)} %copy-done.9), channel_id=1, source_target_pairs={{0,16},{1,17},{2,18},{3,19},{4,20},{5,21},{6,22},{7,23},{8,24},{9,... | collective-permute-start | bytes 2359304 | tf_op jit(solution)/shard_map/ppermute | solution.py:14
  14.5 0.2 fusion.10
  14.8 0.2 fusion.8
  15.1 6.5 %all-gather.9.cloned.1.call-done = bf16[2,384,768]{2,1,0:T(8,128)(2,1)} async-done(((bf16[1,384,768]{2,1,0:T(8,128)(2,1)}), bf16[2,384,768]{2,1,0:T(8,128)(2,1)}) %all-gather.9.cloned.1.call-update) | async-done | bytes 1179664 | tf_op jit(solution)/shard_map/all_gather | solution.py:84
  21.5 3.3 %fusion.39 = f32[512,768]{1,0:T(8,128)} fusion(bf16[768,768]{1,0:T(8,128)(2,1)} %bitcast.46, bf16[512,768]{1,0:T(8,128)(2,1)S(1)} %copy-done.1, f32[512]{0:T(512)S(1)} %add_rsqrt_fusion.3), kind=kOutput, calls=%fused_computation.77 | convolution fusion | flops 605159424 | bytes 3540992 | tf_op jit(solution)/shard_map/dot_general | solution.py:94
  24.8 8.7 %all-gather.7.cloned.1.call-done = bf16[1,768,768]{2,1,0:T(8,128)(2,1)} async-done(((bf16[1,384,768]{2,1,0:T(8,128)(2,1)}), bf16[1,768,768]{2,1,0:T(8,128)(2,1)}) %all-gather.7.cloned.1.call-update) | async-done | bytes 1179664 | tf_op jit(solution)/shard_map/all_gather | solution.py:85
  33.5 2.2 %fusion.15 = f32[512,768]{1,0:T(8,128)S(1)} fusion(bf16[1,768,768]{2,1,0:T(8,128)(2,1)} %all-gather.7.cloned.1.call-done, bf16[512,768]{1,0:T(8,128)(2,1)S(1)} %copy-done.1, f32[512]{0:T(512)S(1)} %add_rsqrt_fusion.3), kind=kOutput, calls=%fused_computation.47 | convolution fusion | flops 605159424 | bytes 3540992 | tf_op jit(solution)/shard_map/dot_general | solution.py:95
  35.7 1.1 %copy-done.13 = f32[512,768]{1,0:T(8,128)} copy-done((f32[512,768]{1,0:T(8,128)}, f32[512,768]{1,0:T(8,128)S(1)}, u32[]{:S(2)}) %copy-start.13) | copy-done | bytes 1572888
  36.9 2.2 %convolution_convert_fusion = bf16[768,768]{1,0:T(8,128)(2,1)} fusion(f32[512,768]{1,0:T(8,128)S(1)} %fusion.15, f32[512,768]{1,0:T(8,128)S(1)} %copy-done.11, bf16[512,768]{1,0:T(8,128)(2,1)S(1)} %copy-done.9, f32[512]{0:T(512)S(1)} %bitcast.52), kind=kOutput, calls=%fused_computation.40 | convolution fusion | flops 608501760 | bytes 5113856 | tf_op jit(solution)/shard_map/dot_general | solution.py:42
  39.0 6.4 %all-gather.5.cloned.1.call-done = bf16[1,768,768]{2,1,0:T(8,128)(2,1)} async-done(((bf16[1,384,768]{2,1,0:T(8,128)(2,1)}), bf16[1,768,768]{2,1,0:T(8,128)(2,1)}) %all-gather.5.cloned.1.call-update) | async-done | bytes 1179664 | tf_op jit(solution)/shard_map/all_gather | solution.py:86
  45.5 2.3 %fusion.18 = f32[512,768]{1,0:T(8,128)S(1)} fusion(bf16[1,768,768]{2,1,0:T(8,128)(2,1)} %all-gather.5.cloned.1.call-done, bf16[512,768]{1,0:T(8,128)(2,1)S(1)} %copy-done.9, f32[512]{0:T(512)S(1)} %bitcast.53), kind=kOutput, calls=%fused_computation.50 | convolution fusion | flops 605552640 | bytes 3540992 | tf_op jit(solution)/shard_map/dot_general | solution.py:48
  47.7 2.2 %convolution_convert_fusion.2 = bf16[768,768]{1,0:T(8,128)(2,1)} fusion(f32[512,768]{1,0:T(8,128)S(1)} %copy-done.12, f32[512,768]{1,0:T(8,128)S(1)} %fusion.18, f32[512,768]{1,0:T(8,128)S(1)} %copy-done.14, bf16[512,768]{1,0:T(8,128)(2,1)S(1)} %copy-done.1, f32[512]{0:T(512)S(1)} %add_rsqrt_fusion.3), kind=kOutput, calls=%fused_computation.42 | convolution fusion | flops 609681408 | bytes 6686720 | tf_op jit(solution)/shard_map/dot_general | solution.py:42
  50.0 2.1 %convolution_convert_fusion.1 = bf16[768,768]{1,0:T(8,128)(2,1)} fusion(f32[512,768]{1,0:T(8,128)S(1)} %fusion.18, f32[512,768]{1,0:T(8,128)S(1)} %copy-done.12, bf16[512,768]{1,0:T(8,128)(2,1)S(1)} %copy-done.1, f32[512]{0:T(512)S(1)} %add_rsqrt_fusion.3), kind=kOutput, calls=%fused_computation.41 | convolution fusion | flops 608108544 | bytes 5113856 | tf_op jit(solution)/shard_map/dot_general | solution.py:42
  52.1 1.2 %copy.24 = bf16[512,768]{0,1:T(8,128)(2,1)} copy(bf16[512,768]{1,0:T(8,128)(2,1)S(1)} %copy-done.2) | data formatting | bytes 1572864 | tf_op args[0]
  53.3 1.6 %compare_and_fusion = pred[512,1024]{0,1:T(8,128)(4,1)} fusion(s32[512]{0:T(512)S(1)} %get-tuple-element.18, s32[512]{0:T(512)S(1)} %get-tuple-element.17, s32[1024]{0:T(1024)S(1)} %iota_add_fusion, pred[1024]{0:T(1024)(128)(4,1)S(1)} %broadcast_compare_fusion), kind=kLoop, calls=%fused_computation.23 | loop fusion | flops 2097152 | bytes 533504 | tf_op jit(solution)/shard_map/and | solution.py:26
  54.8 1.5 %pad_maximum_fusion = bf16[1024,768]{1,0:T(8,128)(2,1)S(1)} fusion(bf16[512,768]{1,0:T(8,128)(2,1)} %param.9, bf16[512,768]{1,0:T(8,128)(2,1)} %collective-permute-done), kind=kLoop, calls=%fused_computation.32 | loop fusion | flops 3145728 | bytes 3145728 | tf_op jit(solution)/shard_map/concatenate | solution.py:76
  56.3 1.7 %copy.21 = bf16[1024,768]{0,1:T(8,128)(2,1)} copy(bf16[1024,768]{1,0:T(8,128)(2,1)S(1)} %pad_maximum_fusion) | data formatting | bytes 3145728 | tf_op jit(solution)/shard_map/concatenate | solution.py:76
  58.0 2.6 %pad_maximum_fusion.1 = bf16[1024,768]{0,1:T(8,128)(2,1)} fusion(bf16[512,768]{0,1:T(8,128)(2,1)S(1)} %copy.22, bf16[512,768]{0,1:T(8,128)(2,1)} %collective-permute-done.1), kind=kLoop, calls=%fused_computation.33 | loop fusion | flops 3145728 | bytes 3145728 | tf_op jit(solution)/shard_map/concatenate | solution.py:73
  60.6 11.1 %fusion.42 = (f32[6,512]{1,0:T(8,128)S(1)}, f32[6,512,1024]{1,2,0:T(8,128)}) fusion(pred[512,1024]{0,1:T(8,128)(4,1)} %compare_and_fusion, bf16[1024,6,128]{0,2,1:T(8,128)(2,1)} %bitcast.49, bf16[512,6,128]{0,2,1:T(8,128)(2,1)S(1)} %bitcast.50), kind=kOutput, calls=%fused_computation.78 | convolution fusion | flops 817890304 | bytes 15478784 | tf_op jit(solution)/shard_map/sub | solution.py:35
  71.7 7.2 %fusion.12 = bf16[6,128,512]{2,1,0:T(8,128)(2,1)S(1)} fusion(bf16[1024,6,128]{0,2,1:T(8,128)(2,1)S(1)} %bitcast.48, f32[6,512,1024]{1,2,0:T(8,128)} %get-tuple-element.16, f32[6,512]{1,0:T(8,128)S(1)} %get-tuple-element.15), kind=kOutput, calls=%fused_computation.44 | convolution fusion | flops 811991040 | bytes 14954496 | tf_op jit(solution)/shard_map/hij,jhd->ihd/dot_general | solution.py:37
  78.9 1.2 %copy.28 = bf16[512,768]{1,0:T(8,128)(2,1)} copy(bf16[512,768]{0,1:T(8,128)(2,1)S(1)} %bitcast.51) | data formatting | bytes 1572864
  80.1 0.2 copy-done
  80.3 0.3 multiply_reduce_fusion
  80.7 1.8 %multiply_reduce_fusion.3 = f32[768]{0:T(1024)S(1)} fusion(bf16[768,768]{1,0:T(8,128)(2,1)} %get-tuple-element.13, bf16[2,384,768]{2,1,0:T(8,128)(2,1)S(1)} %copy-done), kind=kLoop, calls=%fused_computation.21 | loop fusion | flops 2948352 | bytes 2362368 | tf_op jit(solution)/shard_map/reduce_sum | solution.py:57
  82.6 0.2 copy-done.7
  82.8 2.5 %fusion.6 = (f32[768]{0:T(1024)S(1)}, f32[768]{0:T(1024)S(1)}, f32[768]{0:T(1024)S(1)}, f32[768]{0:T(1024)S(1)}) fusion(bf16[1,768,768]{2,1,0:T(8,128)(2,1)S(1)} %copy-done.5, bf16[768,768]{1,0:T(8,128)(2,1)} %get-tuple-element.14, bf16[768,768]{1,0:T(8,128)(2,1)S(1)} %copy-done.7, bf16[1,768,768]{2,1,0:T(8,128)(2,1)S(1)} %copy-done.6), kind=kLoop, calls=%fused_computation.13 | loop fusion | flops 8254464 | bytes 4730880 | tf_op jit(solution)/shard_map/reduce_sum | solution.py:56
  85.3 2.1 %fusion.13 = f32[512,768]{1,0:T(8,128)} fusion(bf16[768,768]{1,0:T(8,128)(2,1)S(1)} %copy-done.4, bf16[768,768]{1,0:T(8,128)(2,1)S(1)} %bitcast.47, f32[768]{0:T(1024)S(1)} %add_rsqrt_fusion.2, f32[768]{0:T(1024)S(1)} %multiply_sqrt_fusion.2, bf16[512,768]{1,0:T(8,128)(2,1)S(1)} %copy-done.2, f32[512]{0:T(512)S(1)} %add_rsqrt_fusion.4), kind=kOutput, calls=%fused_computation.45 | convolution fusion | flops 608698368 | bytes 4726784 | tf_op jit(solution)/shard_map/dot_general | solution.py:62
  87.4 5.1 %convolution_convert_fusion.3 = bf16[512,768]{1,0:T(8,128)(2,1)} fusion(bf16[768,768]{1,0:T(8,128)(2,1)} %get-tuple-element.12, bf16[1,768,768]{2,1,0:T(8,128)(2,1)} %all-gather.5.cloned.1.call-done, f32[768]{0:T(1024)S(1)} %add_rsqrt_fusion, f32[768]{0:T(1024)S(1)} %multiply_sqrt_fusion, f32[512,768]{1,0:T(8,128)} %fusion.13, ...), kind=kOutput, calls=%fused_computation.43 | convolution fusion | flops 1218969600 | bytes 7878656 | tf_op jit(solution)/shard_map/dot_general | solution.py:65
  (47 shorter events, 0.3 us)
Async XLA Ops:
  7.2 1.6 %copy-start.1 = (bf16[512,768]{1,0:T(8,128)(2,1)S(1)}, bf16[512,768]{1,0:T(8,128)(2,1)}, u32[]{:S(2)}) copy-start(bf16[512,768]{1,0:T(8,128)(2,1)} %param.8) | copy-start | bytes 2359300
  7.2 5.1 %copy-start.9 = (bf16[512,768]{1,0:T(8,128)(2,1)S(1)}, bf16[512,768]{1,0:T(8,128)(2,1)}, u32[]{:S(2)}) copy-start(bf16[512,768]{1,0:T(8,128)(2,1)} %param.9) | copy-start | bytes 2359300
  7.2 14.3 %all-gather.9.cloned.1.call-start = ((), (), s32[]{:S(2)}) async-start(), calls=%async_computation.2 | async-start | bytes 1769472 | tf_op jit(solution)/shard_map/all_gather | solution.py:84
  7.9 25.6 %all-gather.7.cloned.1.call-start = ((), (), s32[]{:S(2)}) async-start(), calls=%async_computation.1 | async-start | bytes 1769472 | tf_op jit(solution)/shard_map/all_gather | solution.py:85
  8.7 6.1 %copy-start.2 = (bf16[512,768]{1,0:T(8,128)(2,1)S(1)}, bf16[512,768]{1,0:T(8,128)(2,1)}, u32[]{:S(2)}) copy-start(bf16[512,768]{1,0:T(8,128)(2,1)} %param.7) | copy-start | bytes 2359300
  8.7 36.8 %all-gather.5.cloned.1.call-start = ((), (), s32[]{:S(2)}) async-start(), calls=%async_computation | async-start | bytes 1769472 | tf_op jit(solution)/shard_map/all_gather | solution.py:86
  9.0 49.0 %collective-permute-start.1 = (bf16[512,768]{0,1:T(8,128)(2,1)S(1)}, bf16[512,768]{0,1:T(8,128)(2,1)}, u32[]{:S(2)}, u32[]{:S(2)}) collective-permute-start(bf16[512,768]{0,1:T(8,128)(2,1)S(1)} %copy.22), channel_id=1, source_target_pairs={{0,16},{1,17},{2,18},{3,19},{4,20},{5,21},{6,22},{7,23},{8,24},{9,... | collective-permute-start | bytes 2359304 | tf_op jit(solution)/shard_map/ppermute | solution.py:14
  12.3 42.5 %collective-permute-start = (bf16[512,768]{1,0:T(8,128)(2,1)S(1)}, bf16[512,768]{1,0:T(8,128)(2,1)}, u32[]{:S(2)}, u32[]{:S(2)}) collective-permute-start(bf16[512,768]{1,0:T(8,128)(2,1)S(1)} %copy-done.9), channel_id=1, source_target_pairs={{0,16},{1,17},{2,18},{3,19},{4,20},{5,21},{6,22},{7,23},{8,24},{9,... | collective-permute-start | bytes 2359304 | tf_op jit(solution)/shard_map/ppermute | solution.py:14
  14.5 66.2 %all-reduce.3.cloned.1.call-start = ((), (), s32[]{:S(2)}) async-start(), calls=%async_computation.3 | async-start | bytes 7077888 | tf_op jit(solution)/shard_map/psum | solution.py:109
  24.8 12.1 %copy-start.10 = (f32[512,1]{0,1:T(1,128)S(1)}, f32[512,1]{0,1:T(1,128)}, u32[]{:S(2)}) copy-start(f32[512,1]{0,1:T(1,128)} %param.10) | copy-start | bytes 6148
  33.5 3.4 %copy-start.11 = (f32[512,768]{1,0:T(8,128)S(1)}, f32[512,768]{1,0:T(8,128)}, u32[]{:S(2)}) copy-start(f32[512,768]{1,0:T(8,128)} %fusion.39) | copy-start | bytes 4718596
  35.7 1.1 %copy-start.13 = (f32[512,768]{1,0:T(8,128)}, f32[512,768]{1,0:T(8,128)S(1)}, u32[]{:S(2)}) copy-start(f32[512,768]{1,0:T(8,128)S(1)} %fusion.15) | copy-start | bytes 4718596
  45.5 2.3 %copy-start.12 = (f32[512,768]{1,0:T(8,128)S(1)}, f32[512,768]{1,0:T(8,128)}, u32[]{:S(2)}) copy-start(f32[512,768]{1,0:T(8,128)} %fusion.39) | copy-start | bytes 4718596
  45.5 2.3 %copy-start.14 = (f32[512,768]{1,0:T(8,128)S(1)}, f32[512,768]{1,0:T(8,128)}, u32[]{:S(2)}) copy-start(f32[512,768]{1,0:T(8,128)} %copy-done.13) | copy-start | bytes 4718596
  58.0 2.6 %copy-start.8 = (bf16[512,768]{0,1:T(8,128)(2,1)S(1)}, bf16[512,768]{0,1:T(8,128)(2,1)}, u32[]{:S(2)}) copy-start(bf16[512,768]{0,1:T(8,128)(2,1)} %copy.24) | copy-start | bytes 2359300
  60.6 11.1 %copy-start.3 = (bf16[1024,768]{0,1:T(8,128)(2,1)S(1)}, bf16[1024,768]{0,1:T(8,128)(2,1)}, u32[]{:S(2)}) copy-start(bf16[1024,768]{0,1:T(8,128)(2,1)} %copy.21) | copy-start | bytes 4718596
  78.9 1.4 %copy-start = (bf16[2,384,768]{2,1,0:T(8,128)(2,1)S(1)}, bf16[2,384,768]{2,1,0:T(8,128)(2,1)}, u32[]{:S(2)}) copy-start(bf16[2,384,768]{2,1,0:T(8,128)(2,1)} %all-gather.9.cloned.1.call-done) | copy-start | bytes 3538948
  80.3 2.2 %copy-start.5 = (bf16[1,768,768]{2,1,0:T(8,128)(2,1)S(1)}, bf16[1,768,768]{2,1,0:T(8,128)(2,1)}, u32[]{:S(2)}) copy-start(bf16[1,768,768]{2,1,0:T(8,128)(2,1)} %all-gather.7.cloned.1.call-done) | copy-start | bytes 3538948
  80.7 1.9 %copy-start.6 = (bf16[1,768,768]{2,1,0:T(8,128)(2,1)S(1)}, bf16[1,768,768]{2,1,0:T(8,128)(2,1)}, u32[]{:S(2)}) copy-start(bf16[1,768,768]{2,1,0:T(8,128)(2,1)} %all-gather.5.cloned.1.call-done) | copy-start | bytes 3538948
  80.7 2.1 %copy-start.7 = (bf16[768,768]{1,0:T(8,128)(2,1)S(1)}, bf16[768,768]{1,0:T(8,128)(2,1)}, u32[]{:S(2)}) copy-start(bf16[768,768]{1,0:T(8,128)(2,1)} %get-tuple-element.12) | copy-start | bytes 3538948
  82.8 2.5 %copy-start.4 = (bf16[768,768]{1,0:T(8,128)(2,1)S(1)}, bf16[768,768]{1,0:T(8,128)(2,1)}, u32[]{:S(2)}) copy-start(bf16[768,768]{1,0:T(8,128)(2,1)} %get-tuple-element.13) | copy-start | bytes 3538948
Sparse Core Ops, SparseCore 0:
  9.5 11.9 all-gather.8
  23.1 10.3 all-gather.6
  35.0 10.3 all-gather.4
  52.2 25.4 all-reduce.2
